TPU v7x, 32 devices: a whole 2x2x4 slice. The times are simulated.
32 devices in a mesh: lon: 8 (over y, x, core), lat: 4 (over z).
Axes of the slice: x: 2, y: 2, z: 4, core: 2. Of those that a mesh axis runs over, the one named last changes fastest.
Arguments:
- fields: float32 [5, 1, 128, 11520], P(None, None, 'lat', 'lon'), may hold values from -6 to 6
- frac_x: float32 [2, 1, 128], replicated, may hold values from 0.05 to 0.95
- frac_y: float32 [2, 1, 128], replicated, may hold values from 0.05 to 0.9
- shift_cells: int32 [2, 1, 128], replicated, may hold values from -5760 to 5759, as said below
- polar_mask: int32 [128], replicated, may hold values from 0 to 1, as said below
Outputs:
- fields_out: float32 [5, 1, 128, 11520], P(None, None, 'lat', 'lon')
Inputs may be any that keep to these rules, and one draw needn't show every extreme that they name: `shift_cells`: outside the first and last 32 rows every count lies in -2 .. 1, and both -2 and 1 occur there. `polar_mask`: nonzero only in the first and last 32 rows; the first and the last row are 1.
All inputs are finite; a program needn't handle non-finite values.
Results may differ from a plain program's by a relative error of at most 0.00016.
Values sent between devices are 32-bit elements; how exact they have to be, the bound alone decides.
A program may use at most 64 MiB of HBM per device.

v0:
```python
import math
import jax
import jax.numpy as jnp
from jax import lax
from jax.sharding import PartitionSpec as P

FA = 90
FB = 128
SUBS = 2
REACH = 4


def passed_along(x, axis, by):
    devices = lax.axis_size(axis)
    return lax.ppermute(x, axis, [(i, (i + by) % devices) for i in range(devices)])


def passed_along_2(block, axis, distance):
    devices = range(lax.axis_size(axis))
    route = [(i - distance, i) for i in devices if i - distance in devices]
    return lax.ppermute(block, axis, route)


def roll_digits(values, amount, span, axis):
    bit_total = max((span - 1).bit_length(), 1)
    for bit in range(bit_total):
        moved = jnp.roll(values, 1 << bit, axis=axis)
        taken = amount >> bit & 1 == 1
        values = jnp.where(taken, moved, values)
    return values


def cycle_move(state, counts, lon_cells):
    device_jump = jnp.floor_divide(counts, lon_cells)
    remainder = counts - device_jump * lon_cells
    select = device_jump + REACH
    bit_count = (2 * REACH).bit_length() - 1
    offsets = [-REACH] + [1 << bit for bit in range(bit_count)]
    current = state
    for turn, offset in enumerate(offsets):
        moved = passed_along(current, "lon", offset)
        if turn == 0:
            current = moved
        else:
            taken = select >> turn - 1 & 1 == 1
            current = jnp.where(taken[None, :, :, None], moved, current)
    western = passed_along(current, "lon", 1)
    joined = jnp.concatenate([western, current], axis=3)
    rolled = roll_digits(joined, remainder[None, :, :, None], lon_cells, 3)
    return rolled[:, :, :, lon_cells:]


def zonal_fraction(whole, courant):
    previous = jnp.roll(whole, 1, axis=1)
    edge = whole + 0.5 * (1.0 - courant) * (whole - previous)
    return whole - courant * (edge - jnp.roll(edge, 1, axis=1))


def polar_smooth(whole, lat_rows, marks, lat_cells, lat_total):
    row_count, lon_total = whole.shape
    highest = lax.Precision.HIGHEST
    first_ids = jnp.arange(FA, dtype=jnp.int32)
    second_ids = jnp.arange(FB, dtype=jnp.int32)
    angle_first = (
        2.0 * math.pi * (first_ids[:, None] * first_ids[None, :] % FA).astype(jnp.float32) / FA
    )
    cos_first, sin_first = (jnp.cos(angle_first), jnp.sin(angle_first))
    angle_second = (
        2.0 * math.pi * (second_ids[:, None] * second_ids[None, :] % FB).astype(jnp.float32) / FB
    )
    cos_second, sin_second = (jnp.cos(angle_second), jnp.sin(angle_second))
    angle_twist = (
        2.0
        * math.pi
        * (first_ids[:, None] * second_ids[None, :] % lon_total).astype(jnp.float32)
        / lon_total
    )
    cos_twist, sin_twist = (jnp.cos(angle_twist), jnp.sin(angle_twist))
    waves = (first_ids[:, None] + FA * second_ids[None, :]).astype(jnp.float32)
    sine = jnp.sin(math.pi * waves / lon_total)
    phi = math.pi * (lat_rows.astype(jnp.float32) + 0.5) / lat_total - math.pi / 2
    edge_cos = math.sin(math.pi * (lat_cells - 0.5) / lat_total)
    b_val = jnp.cos(phi) / edge_cos
    gain = 1.0 / (1.0 + sine[None, :, :] ** 2 / b_val[:, None, None] ** 2)
    grid = whole.reshape(row_count, FA, FB)
    real_one = jnp.einsum("kn,rnm->rkm", cos_first, grid, precision=highest)
    imag_one = -jnp.einsum("kn,rnm->rkm", sin_first, grid, precision=highest)
    real_two = real_one * cos_twist + imag_one * sin_twist
    imag_two = imag_one * cos_twist - real_one * sin_twist
    real_spec = jnp.einsum("rkm,mq->rkq", real_two, cos_second, precision=highest) + jnp.einsum(
        "rkm,mq->rkq", imag_two, sin_second, precision=highest
    )
    imag_spec = jnp.einsum("rkm,mq->rkq", imag_two, cos_second, precision=highest) - jnp.einsum(
        "rkm,mq->rkq", real_two, sin_second, precision=highest
    )
    real_spec = real_spec * gain
    imag_spec = imag_spec * gain
    real_back = jnp.einsum("rkq,mq->rkm", real_spec, cos_second, precision=highest) - jnp.einsum(
        "rkq,mq->rkm", imag_spec, sin_second, precision=highest
    )
    imag_back = jnp.einsum("rkq,mq->rkm", imag_spec, cos_second, precision=highest) + jnp.einsum(
        "rkq,mq->rkm", real_spec, sin_second, precision=highest
    )
    real_turn = real_back * cos_twist - imag_back * sin_twist
    imag_turn = imag_back * cos_twist + real_back * sin_twist
    result = jnp.einsum("kn,rkm->rnm", cos_first, real_turn, precision=highest) - jnp.einsum(
        "kn,rkm->rnm", sin_first, imag_turn, precision=highest
    )
    result = result.reshape(row_count, lon_total) / lon_total
    return jnp.where((marks == 1)[:, None], result, whole)


def meridional(state, merid_step, first_row):
    n_fields, n_levels, lat_cells, lon_cells = state.shape
    southern = passed_along_2(state[:, :, lat_cells - 2 :, :], "lat", 1)
    extended = jnp.concatenate([southern, state], axis=2)
    padded_faces = jnp.concatenate([merid_step, jnp.zeros((n_levels, 1), jnp.float32)], axis=1)
    faces = lax.dynamic_slice_in_dim(padded_faces, first_row, lat_cells + 1, 1)
    face_ids = first_row + jnp.arange(lat_cells + 1, dtype=jnp.int32)
    faces = jnp.where((face_ids == 0)[None, :], jnp.zeros_like(faces), faces)
    courant = faces[None, :, :, None]
    upper = extended[:, :, 1 : lat_cells + 2, :]
    lower = extended[:, :, 0 : lat_cells + 1, :]
    flux = courant * (upper + 0.5 * (1.0 - courant) * (upper - lower))
    return state + flux[:, :, :lat_cells, :] - flux[:, :, 1:, :]


def body(fields, frac_x, frac_y, shift_cells, polar_mask):
    n_fields, n_levels, lat_cells, lon_cells = fields.shape
    lon_devs = lax.axis_size("lon")
    lat_total = lat_cells * lax.axis_size("lat")
    lon_index = lax.axis_index("lon")
    first_row = lax.axis_index("lat") * lat_cells
    row_total = n_fields * n_levels * lat_cells
    per_device = row_total // lon_devs
    row_start = lon_index * per_device
    local_rows = first_row + jnp.arange(lat_cells, dtype=jnp.int32)
    marks_local = lax.dynamic_slice_in_dim(polar_mask, first_row, lat_cells, 0)

    def my_rows(table):
        spread = jnp.broadcast_to(table[None], (n_fields, n_levels, lat_cells)).reshape(row_total)
        return lax.dynamic_slice_in_dim(spread, row_start, per_device, 0)

    row_lats = my_rows(local_rows[None])
    row_marks = my_rows(marks_local[None])
    state = fields
    for substep in range(SUBS):
        counts = lax.dynamic_slice_in_dim(shift_cells[substep], first_row, lat_cells, 1)
        fractions = lax.dynamic_slice_in_dim(frac_x[substep], first_row, lat_cells, 1)
        placed = cycle_move(state, counts, lon_cells)
        flat = placed.reshape(row_total, lon_cells)
        whole = lax.all_to_all(flat, "lon", split_axis=0, concat_axis=1, tiled=True)
        whole = zonal_fraction(whole, my_rows(fractions)[:, None])
        whole = polar_smooth(whole, row_lats, row_marks, lat_cells, lat_total)
        blocks = lax.all_to_all(whole, "lon", split_axis=1, concat_axis=0, tiled=True)
        state = blocks.reshape(n_fields, n_levels, lat_cells, lon_cells)
        state = meridional(state, frac_y[substep], first_row)
    return state


def solution(mesh):
    return jax.shard_map(
        body,
        mesh=mesh,
        in_specs=(P(None, None, "lat", "lon"), P(), P(), P(), P()),
        out_specs=P(None, None, "lat", "lon"),
        check_vma=False,
    )
```

profile of v0, /device:TPU:0, one launch (start us, length us, event | category | flops | bytes accessed | tf_op | source)
XLA Modules:
  0.0 374.6 jit_solution(14722888508883360047)
XLA Ops:
  0.0 3.0 collective-permute-start
  3.0 22.0 %collective-permute-done = f32[5,1,32,1440]{3,2,1,0:T(8,128)S(1)} collective-permute-done((f32[5,1,32,1440]{3,2,1,0:T(8,128)}, f32[5,1,32,1440]{3,2,1,0:T(8,128)S(1)}, u32[]{:S(2)}, u32[]{:S(2)}) %collective-permute-start) | collective-permute-done | bytes 921632 | tf_op jit(solution)/shard_map/ppermute | solution.py:15
  26.3 13.1 %collective-permute-done.1 = f32[5,1,32,1440]{3,2,1,0:T(8,128)S(1)} collective-permute-done((f32[5,1,32,1440]{3,2,1,0:T(8,128)S(1)}, f32[5,1,32,1440]{3,2,1,0:T(8,128)S(1)}, u32[]{:S(2)}, u32[]{:S(2)}) %collective-permute-start.1) | collective-permute-done | bytes 921632 | tf_op jit(solution)/shard_map/ppermute | solution.py:15
  40.4 22.2 %collective-permute-done.2 = f32[5,1,32,1440]{3,2,1,0:T(8,128)S(1)} collective-permute-done((f32[5,1,32,1440]{3,2,1,0:T(8,128)S(1)}, f32[5,1,32,1440]{3,2,1,0:T(8,128)S(1)}, u32[]{:S(2)}, u32[]{:S(2)}) %collective-permute-start.2) | collective-permute-done | bytes 921632 | tf_op jit(solution)/shard_map/ppermute | solution.py:15
  62.8 1.6 collective-permute-start.3
  64.4 19.7 %collective-permute-done.3 = f32[5,1,32,1440]{3,2,1,0:T(8,128)S(1)} collective-permute-done((f32[5,1,32,1440]{3,2,1,0:T(8,128)S(1)}, f32[5,1,32,1440]{3,2,1,0:T(8,128)S(1)}, u32[]{:S(2)}, u32[]{:S(2)}) %collective-permute-start.3) | collective-permute-done | bytes 921632 | tf_op jit(solution)/shard_map/ppermute | solution.py:15
  85.2 13.6 %collective-permute-done.4 = f32[5,1,32,1440]{3,2,1,0:T(8,128)S(1)} collective-permute-done((f32[5,1,32,1440]{3,2,1,0:T(8,128)S(1)}, f32[5,1,32,1440]{3,2,1,0:T(8,128)S(1)}, u32[]{:S(2)}, u32[]{:S(2)}) %collective-permute-start.4) | collective-permute-done | bytes 921632 | tf_op jit(solution)/shard_map/ppermute | solution.py:15
  106.3 1.2 all_to_all.52
  107.5 3.8 %all-to-all-start = ((f32[8,20,1440]{2,1,0:T(8,128)}), f32[8,20,1440]{2,1,0:T(8,128)S(1)}, u32[]{:S(2)}, u32[]{:S(2)}) async-start(f32[8,20,1440]{2,1,0:T(8,128)} %all_to_all.52), calls=%async_computation | async-start | bytes 2359296 | tf_op jit(solution)/shard_map/all_to_all | solution.py:152
  112.8 15.0 %all-to-all-done = f32[8,20,1440]{2,1,0:T(8,128)S(1)} async-done(((f32[8,20,1440]{2,1,0:T(8,128)}), f32[8,20,1440]{2,1,0:T(8,128)S(1)}, u32[]{:S(2)}, u32[]{:S(2)}) %all-to-all-start) | async-done | bytes 921632 | tf_op jit(solution)/shard_map/all_to_all | solution.py:152
  128.4 1.4 all_to_all.55
  131.2 1.6 concatenate.853
  132.9 1.2 concatenate.851
  134.1 1.6 concatenate.852
  136.8 2.1 multiply_subtract_fusion.3
  138.9 1.2 fusion.13
  140.1 1.2 convolution_bitcast_fusion.1
  141.3 1.2 fusion.55
  142.5 1.2 fusion.54
  143.7 1.2 fusion.11
  144.9 1.6 fusion.75
  146.5 1.2 fusion.12
  147.7 1.2 fusion.78
  148.8 1.2 convolution_add_fusion.2
  150.0 1.2 convolution_subtract_fusion.4
  151.2 1.3 fusion.42
  152.5 2.3 fusion.10
  154.8 2.9 div.293
  157.7 4.0 %copy_select_fusion.1 = f32[20,8,1440]{2,0,1:T(8,128)} fusion(f32[20,8,1440]{2,1,0:T(8,128)} %div.293, f32[20,8,1440]{2,1,0:T(8,128)S(1)} %copy-done.2, f32[20,8,1440]{2,1,0:T(8,128)S(1)} %copy-done.3, f32[20]{0:T(128)S(1)} %get-tuple-element.18, f32[20]{0:T(128)S(1)} %get-tuple-element.19, pred[20]{0:T(512)(128)(4,1)S(1)} %dynamic-slice_compare_fusion, ...), kind=kLoop, calls=%fused_computation.69 | loop fusion | flops 1612800 | bytes 4608180 | tf_op jit(solution)/shard_map/jit(_where)/select_n | solution.py:110
  161.7 3.7 all-to-all-start.1
  166.0 16.2 %all-to-all-done.1 = f32[20,8,1440]{2,0,1:T(8,128)S(1)} async-done(((f32[20,8,1440]{2,0,1:T(8,128)}), f32[20,8,1440]{2,0,1:T(8,128)S(1)}, u32[]{:S(2)}, u32[]{:S(2)}) %all-to-all-start.1) | async-done | bytes 921632 | tf_op jit(solution)/shard_map/all_to_all | solution.py:155
  182.3 3.3 collective-permute-start.5
  185.6 1.8 collective-permute-done.5
  188.6 19.2 %collective-permute-done.6 = f32[5,1,32,1440]{3,2,0,1:T(8,128)S(1)} collective-permute-done((f32[5,1,32,1440]{3,2,0,1:T(8,128)S(1)}, f32[5,1,32,1440]{3,2,0,1:T(8,128)S(1)}, u32[]{:S(2)}, u32[]{:S(2)}) %collective-permute-start.6) | collective-permute-done | bytes 921632 | tf_op jit(solution)/shard_map/ppermute | solution.py:15
  207.9 14.4 %collective-permute-done.7 = f32[5,1,32,1440]{3,2,0,1:T(8,128)S(1)} collective-permute-done((f32[5,1,32,1440]{3,2,0,1:T(8,128)S(1)}, f32[5,1,32,1440]{3,2,0,1:T(8,128)S(1)}, u32[]{:S(2)}, u32[]{:S(2)}) %collective-permute-start.7) | collective-permute-done | bytes 921632 | tf_op jit(solution)/shard_map/ppermute | solution.py:15
  222.5 2.9 collective-permute-start.8
  225.4 22.2 %collective-permute-done.8 = f32[5,1,32,1440]{3,2,0,1:T(8,128)S(1)} collective-permute-done((f32[5,1,32,1440]{3,2,0,1:T(8,128)S(1)}, f32[5,1,32,1440]{3,2,0,1:T(8,128)S(1)}, u32[]{:S(2)}, u32[]{:S(2)}) %collective-permute-start.8) | collective-permute-done | bytes 921632 | tf_op jit(solution)/shard_map/ppermute | solution.py:15
  248.2 22.8 %collective-permute-done.9 = f32[5,1,32,1440]{3,2,0,1:T(8,128)S(1)} collective-permute-done((f32[5,1,32,1440]{3,2,0,1:T(8,128)S(1)}, f32[5,1,32,1440]{3,2,0,1:T(8,128)S(1)}, u32[]{:S(2)}, u32[]{:S(2)}) %collective-permute-start.9) | collective-permute-done | bytes 921632 | tf_op jit(solution)/shard_map/ppermute | solution.py:15
  271.4 14.3 %collective-permute-done.10 = f32[5,1,32,1440]{3,2,0,1:T(8,128)S(1)} collective-permute-done((f32[5,1,32,1440]{3,2,0,1:T(8,128)S(1)}, f32[5,1,32,1440]{3,2,0,1:T(8,128)S(1)}, u32[]{:S(2)}, u32[]{:S(2)}) %collective-permute-start.10) | collective-permute-done | bytes 921632 | tf_op jit(solution)/shard_map/ppermute | solution.py:15
  293.3 1.2 all_to_all.59
  294.5 3.8 %all-to-all-start.2 = ((f32[8,20,1440]{2,1,0:T(8,128)}), f32[8,20,1440]{2,1,0:T(8,128)S(1)}, u32[]{:S(2)}, u32[]{:S(2)}) async-start(f32[8,20,1440]{2,1,0:T(8,128)} %all_to_all.59), calls=%async_computation.2 | async-start | bytes 2359296 | tf_op jit(solution)/shard_map/all_to_all | solution.py:152
  298.4 16.3 %all-to-all-done.2 = f32[8,20,1440]{2,1,0:T(8,128)S(1)} async-done(((f32[8,20,1440]{2,1,0:T(8,128)}), f32[8,20,1440]{2,1,0:T(8,128)S(1)}, u32[]{:S(2)}, u32[]{:S(2)}) %all-to-all-start.2) | async-done | bytes 921632 | tf_op jit(solution)/shard_map/all_to_all | solution.py:152
  315.3 1.4 all_to_all.62
  318.2 1.6 concatenate.873
  319.8 1.2 concatenate.871
  321.0 1.6 concatenate.872
  323.8 2.1 multiply_subtract_fusion.1
  325.9 1.2 fusion.8
  327.0 1.2 convolution_bitcast_fusion
  328.2 1.2 fusion.57
  329.4 1.2 fusion.56
  330.6 1.2 fusion.6
  331.8 1.2 fusion.69
  333.0 1.4 fusion.7
  334.4 1.2 fusion.72
  335.6 1.2 convolution_add_fusion
  336.8 1.2 convolution_subtract_fusion.1
  338.0 1.3 fusion.35
  339.3 2.3 fusion.5
  341.6 2.9 div.296
  344.5 2.9 copy_select_fusion
  347.5 19.2 %all_to_all.70 = f32[20,8,1440]{2,0,1:T(8,128)S(1)} all-to-all(f32[20,8,1440]{2,0,1:T(8,128)S(1)} %copy_select_fusion), channel_id=1, replica_groups=mesh['lon'=8,'lat'=4] {'lon'}, dimensions={1} | all-to-all | bytes 1843200 | tf_op jit(solution)/shard_map/all_to_all | solution.py:155
  366.8 4.0 %collective-permute-start.11 = (f32[5,1,2,1440]{3,2,0,1:T(2,128)S(1)}, f32[5,1,2,1440]{3,2,0,1:T(2,128)S(1)}, u32[]{:S(2)}, u32[]{:S(2)}) collective-permute-start(f32[5,1,2,1440]{3,2,0,1:T(2,128)S(1)} %slice.367), channel_id=1, source_target_pairs={{0,1},{1,2},{2,3},{4,5},{5,6},{6,7},{8,9},{9,10},{10,11},{12,13},{... | collective-permute-start | bytes 172808 | tf_op jit(solution)/shard_map/ppermute | solution.py:21
  370.8 1.8 collective-permute-done.11
  (148 shorter events, 31.3 us)
Async XLA Ops:
  0.0 24.9 %collective-permute-start = (f32[5,1,32,1440]{3,2,1,0:T(8,128)}, f32[5,1,32,1440]{3,2,1,0:T(8,128)S(1)}, u32[]{:S(2)}, u32[]{:S(2)}) collective-permute-start(f32[5,1,32,1440]{3,2,1,0:T(8,128)} %param.5), channel_id=1, source_target_pairs={{0,16},{4,20},{8,24},{12,28},{16,0},{20,4},{24,8},{28,12},{1,17},{... | collective-permute-start | bytes 2764808 | tf_op jit(solution)/shard_map/ppermute | solution.py:15
  24.9 14.4 %collective-permute-start.1 = (f32[5,1,32,1440]{3,2,1,0:T(8,128)S(1)}, f32[5,1,32,1440]{3,2,1,0:T(8,128)S(1)}, u32[]{:S(2)}, u32[]{:S(2)}) collective-permute-start(f32[5,1,32,1440]{3,2,1,0:T(8,128)S(1)} %collective-permute-done), channel_id=1, source_target_pairs={{0,4},{4,8},{8,12},{12,16},{16,20},{20,24},{24,28},{28,0},{1,5},{5... | collective-permute-start | bytes 2764808 | tf_op jit(solution)/shard_map/ppermute | solution.py:15
  39.6 23.1 %collective-permute-start.2 = (f32[5,1,32,1440]{3,2,1,0:T(8,128)S(1)}, f32[5,1,32,1440]{3,2,1,0:T(8,128)S(1)}, u32[]{:S(2)}, u32[]{:S(2)}) collective-permute-start(f32[5,1,32,1440]{3,2,1,0:T(8,128)S(1)} %broadcast_select_fusion), channel_id=1, source_target_pairs={{0,8},{4,12},{8,16},{12,20},{16,24},{20,28},{24,0},{28,4},{1,9},{5... | collective-permute-start | bytes 2764808 | tf_op jit(solution)/shard_map/ppermute | solution.py:15
  62.8 21.5 %copy-start.12 = (s32[128]{0:T(128)S(1)}, s32[128]{0:T(128)}, u32[]{:S(2)}) copy-start(s32[128]{0:T(128)} %param.9) | copy-start | bytes 1540
  62.8 21.6 %copy-start.10 = (f32[2,1,128]{2,1,0:T(1,128)S(1)}, f32[2,1,128]{2,1,0:T(1,128)}, u32[]{:S(2)}) copy-start(f32[2,1,128]{2,1,0:T(1,128)} %param.6) | copy-start | bytes 3076
  62.8 21.3 %collective-permute-start.3 = (f32[5,1,32,1440]{3,2,1,0:T(8,128)S(1)}, f32[5,1,32,1440]{3,2,1,0:T(8,128)S(1)}, u32[]{:S(2)}, u32[]{:S(2)}) collective-permute-start(f32[5,1,32,1440]{3,2,1,0:T(8,128)S(1)} %broadcast_select_fusion.1), channel_id=1, source_target_pairs={{0,16},{4,20},{8,24},{12,28},{16,0},{20,4},{24,8},{28,12},{1,17},{... | collective-permute-start | bytes 2764808 | tf_op jit(solution)/shard_map/ppermute | solution.py:15
  84.3 14.5 %collective-permute-start.4 = (f32[5,1,32,1440]{3,2,1,0:T(8,128)S(1)}, f32[5,1,32,1440]{3,2,1,0:T(8,128)S(1)}, u32[]{:S(2)}, u32[]{:S(2)}) collective-permute-start(f32[5,1,32,1440]{3,2,1,0:T(8,128)S(1)} %broadcast_select_fusion.2), channel_id=1, source_target_pairs={{0,4},{4,8},{8,12},{12,16},{16,20},{20,24},{24,28},{28,0},{1,5},{5... | collective-permute-start | bytes 2764808 | tf_op jit(solution)/shard_map/ppermute | solution.py:15
  107.5 20.3 %all-to-all-start = ((f32[8,20,1440]{2,1,0:T(8,128)}), f32[8,20,1440]{2,1,0:T(8,128)S(1)}, u32[]{:S(2)}, u32[]{:S(2)}) async-start(f32[8,20,1440]{2,1,0:T(8,128)} %all_to_all.52), calls=%async_computation | async-start | bytes 2359296 | tf_op jit(solution)/shard_map/all_to_all | solution.py:152
  134.0 2.8 copy-start.4
  142.4 1.2 copy-start.13
  154.8 2.9 copy-start.2
  154.8 2.9 copy-start.3
  161.7 3.7 copy-start.11
  161.7 20.4 %all-to-all-start.1 = ((f32[20,8,1440]{2,0,1:T(8,128)}), f32[20,8,1440]{2,0,1:T(8,128)S(1)}, u32[]{:S(2)}, u32[]{:S(2)}) async-start(f32[20,8,1440]{2,0,1:T(8,128)} %copy_select_fusion.1), calls=%async_computation.1 | async-start | bytes 2359296 | tf_op jit(solution)/shard_map/all_to_all | solution.py:155
  182.3 5.1 %collective-permute-start.5 = (f32[5,1,2,1440]{3,2,0,1:T(2,128)S(1)}, f32[5,1,2,1440]{3,2,0,1:T(2,128)S(1)}, u32[]{:S(2)}, u32[]{:S(2)}) collective-permute-start(f32[5,1,2,1440]{3,2,0,1:T(2,128)S(1)} %slice.334), channel_id=1, source_target_pairs={{0,1},{1,2},{2,3},{4,5},{5,6},{6,7},{8,9},{9,10},{10,11},{12,13},{... | collective-permute-start | bytes 172808 | tf_op jit(solution)/shard_map/ppermute | solution.py:21
  187.8 20.1 %copy-start.7 = (s32[32]{0:T(128)S(1)}, s32[32]{0:T(128)}, u32[]{:S(2)}) copy-start(s32[32]{0:T(128)} %get-tuple-element.57) | copy-start | bytes 388
  188.0 19.8 %collective-permute-start.6 = (f32[5,1,32,1440]{3,2,0,1:T(8,128)S(1)}, f32[5,1,32,1440]{3,2,0,1:T(8,128)S(1)}, u32[]{:S(2)}, u32[]{:S(2)}) collective-permute-start(f32[5,1,32,1440]{3,2,0,1:T(8,128)S(1)} %slice_subtract_fusion.1), channel_id=1, source_target_pairs={{0,16},{4,20},{8,24},{12,28},{16,0},{20,4},{24,8},{28,12},{1,17},{... | collective-permute-start | bytes 2764808 | tf_op jit(solution)/shard_map/ppermute | solution.py:15
  207.9 14.4 %collective-permute-start.7 = (f32[5,1,32,1440]{3,2,0,1:T(8,128)S(1)}, f32[5,1,32,1440]{3,2,0,1:T(8,128)S(1)}, u32[]{:S(2)}, u32[]{:S(2)}) collective-permute-start(f32[5,1,32,1440]{3,2,0,1:T(8,128)S(1)} %collective-permute-done.6), channel_id=1, source_target_pairs={{0,4},{4,8},{8,12},{12,16},{16,20},{20,24},{24,28},{28,0},{1,5},{5... | collective-permute-start | bytes 2764808 | tf_op jit(solution)/shard_map/ppermute | solution.py:15
  222.5 25.1 %collective-permute-start.8 = (f32[5,1,32,1440]{3,2,0,1:T(8,128)S(1)}, f32[5,1,32,1440]{3,2,0,1:T(8,128)S(1)}, u32[]{:S(2)}, u32[]{:S(2)}) collective-permute-start(f32[5,1,32,1440]{3,2,0,1:T(8,128)S(1)} %broadcast_select_fusion.3), channel_id=1, source_target_pairs={{0,8},{4,12},{8,16},{12,20},{16,24},{20,28},{24,0},{28,4},{1,9},{5... | collective-permute-start | bytes 2764808 | tf_op jit(solution)/shard_map/ppermute | solution.py:15
  247.8 23.5 %copy-start.8 = (s32[32]{0:T(128)S(1)}, s32[32]{0:T(128)}, u32[]{:S(2)}) copy-start(s32[32]{0:T(128)} %get-tuple-element.56) | copy-start | bytes 388
  247.8 23.3 %collective-permute-start.9 = (f32[5,1,32,1440]{3,2,0,1:T(8,128)S(1)}, f32[5,1,32,1440]{3,2,0,1:T(8,128)S(1)}, u32[]{:S(2)}, u32[]{:S(2)}) collective-permute-start(f32[5,1,32,1440]{3,2,0,1:T(8,128)S(1)} %broadcast_select_fusion.4), channel_id=1, source_target_pairs={{0,16},{4,20},{8,24},{12,28},{16,0},{20,4},{24,8},{28,12},{1,17},{... | collective-permute-start | bytes 2764808 | tf_op jit(solution)/shard_map/ppermute | solution.py:15
  271.3 14.5 %collective-permute-start.10 = (f32[5,1,32,1440]{3,2,0,1:T(8,128)S(1)}, f32[5,1,32,1440]{3,2,0,1:T(8,128)S(1)}, u32[]{:S(2)}, u32[]{:S(2)}) collective-permute-start(f32[5,1,32,1440]{3,2,0,1:T(8,128)S(1)} %broadcast_select_fusion.5), channel_id=1, source_target_pairs={{0,4},{4,8},{8,12},{12,16},{16,20},{20,24},{24,28},{28,0},{1,5},{5... | collective-permute-start | bytes 2764808 | tf_op jit(solution)/shard_map/ppermute | solution.py:15
  293.3 5.0 %copy-start.6 = (f32[32]{0:T(128)S(1)}, f32[32]{0:T(128)}, u32[]{:S(2)}) copy-start(f32[32]{0:T(128)} %get-tuple-element.61) | copy-start | bytes 388
  294.5 20.3 %all-to-all-start.2 = ((f32[8,20,1440]{2,1,0:T(8,128)}), f32[8,20,1440]{2,1,0:T(8,128)S(1)}, u32[]{:S(2)}, u32[]{:S(2)}) async-start(f32[8,20,1440]{2,1,0:T(8,128)} %all_to_all.59), calls=%async_computation.2 | async-start | bytes 2359296 | tf_op jit(solution)/shard_map/all_to_all | solution.py:152
  321.0 2.8 copy-start.5
  329.4 1.2 copy-start.14
  341.6 2.9 copy-start
  341.6 2.9 copy-start.1
  347.4 23.3 %copy-start.9 = (f32[1,128]{1,0:T(1,128)S(1)}, f32[1,128]{1,0:T(1,128)}, u32[]{:S(2)}) copy-start(f32[1,128]{1,0:T(1,128)} %get-tuple-element.23) | copy-start | bytes 1540
  366.8 5.8 %collective-permute-start.11 = (f32[5,1,2,1440]{3,2,0,1:T(2,128)S(1)}, f32[5,1,2,1440]{3,2,0,1:T(2,128)S(1)}, u32[]{:S(2)}, u32[]{:S(2)}) collective-permute-start(f32[5,1,2,1440]{3,2,0,1:T(2,128)S(1)} %slice.367), channel_id=1, source_target_pairs={{0,1},{1,2},{2,3},{4,5},{5,6},{6,7},{8,9},{9,10},{10,11},{12,13},{... | collective-permute-start | bytes 172808 | tf_op jit(solution)/shard_map/ppermute | solution.py:21
where the time goes:
time: 381 us; the launch traced here: 375 us
  waiting for transfers between devices  234 us (61%)
  matrix products  31.4 us (8%)
  local copies, waits for them, and re-layouts  30.5 us (8%)
  other arithmetic  29.7 us (8%)
  starting transfers between devices  27.9 us (7%)
  blocking collectives  19.2 us (5%)
    ppermute x10, waiting for transfers between devices, passed_along(): lax.ppermute(x, axis, [(i, (i + by) % devices) for i in range(devices)])  183 us
    all_to_all x2, waiting for transfers between devices, body(): whole = lax.all_to_all(flat, 'lon', split_axis=0, concat_axis=1, tiled=True)  31.3 us
    all_to_all x1, blocking collectives, body(): lax.all_to_all(whole, 'lon', split_axis=1, concat_axis=0, tiled=True)  19.2 us
    all_to_all x1, waiting for transfers between devices, body(): lax.all_to_all(whole, 'lon', split_axis=1, concat_axis=0, tiled=True)  16.2 us
    select_n x22, other arithmetic, roll_digits(): values = jnp.where(taken, moved, values)  11.1 us
    ppermute x10, starting transfers between devices, passed_along(): lax.ppermute(x, axis, [(i, (i + by) % devices) for i in range(devices)])  9.47 us
  transfers between devices with their start and end apart: 15, of which 15 were waited for; matrix products, arithmetic and copies ran while one was open for 1% of the time, Pallas kernels for 0%

commit v1 on v0

--- a/solution.py
+++ b/solution.py
@@ -152,7 +152,15 @@
         whole = lax.all_to_all(flat, "lon", split_axis=0, concat_axis=1, tiled=True)
         whole = zonal_fraction(whole, my_rows(fractions)[:, None])
         whole = polar_smooth(whole, row_lats, row_marks, lat_cells, lat_total)
-        blocks = lax.all_to_all(whole, "lon", split_axis=1, concat_axis=0, tiled=True)
+        ways, here = (lax.axis_size("lon"), lax.axis_index("lon"))
+        width = whole.shape[1] // ways
+        turned = jnp.roll(whole, -here * width, axis=1)
+        got = [lax.slice_in_dim(turned, 0, width, axis=1)]
+        for far in range(1, ways):
+            sent = lax.slice_in_dim(turned, far * width, (far + 1) * width, axis=1)
+            got.append(lax.ppermute(sent, "lon", [(d, (d + far) % ways) for d in range(ways)]))
+        line = jnp.concatenate(got[::-1], axis=0)
+        blocks = jnp.roll(line, (here + 1) * got[0].shape[0], axis=0)
         state = blocks.reshape(n_fields, n_levels, lat_cells, lon_cells)
         state = meridional(state, frac_y[substep], first_row)
     return state

time: 381 us -> 366 us (0.961)
  blocking collectives: 19.2 us -> 0 us
  waiting for transfers between devices: 234 us -> 244 us
  local copies, waits for them, and re-layouts: 30.5 us -> 22.9 us
  starting transfers between devices: 27.9 us -> 35.3 us
    ppermute x0 -> x14, waiting for transfers between devices: none -> 21.6 us  [body(): lax.ppermute(sent, 'lon', [(d, (d + far) % ways) for d in range(ways)])]
    all_to_all x1 -> x0, blocking collectives: 19.2 us -> none  [body(): lax.all_to_all(whole, 'lon', split_axis=1, concat_axis=0, tiled=True)]
    all_to_all x1 -> x0, waiting for transfers between devices: 16.2 us -> none  [body(): lax.all_to_all(whole, 'lon', split_axis=1, concat_axis=0, tiled=True)]
    ppermute x0 -> x14, starting transfers between devices: none -> 11 us  [body(): lax.ppermute(sent, 'lon', [(d, (d + far) % ways) for d in range(ways)])]
    select_n x2, other arithmetic: 6.9 us -> 0.83 us  [polar_smooth(): return jnp.where((marks == 1)[:, None], result, whole)]
    div x2 -> x0, local copies, waits for them, and re-layouts: 5.86 us -> none  [polar_smooth(): result = result.reshape(row_count, lon_total) / lon_total]
  transfers between devices with their start and end apart: 15 -> 28, of which waited for: 15 -> 23; matrix products, arithmetic and copies ran while one was open for 1% -> 1% of each run, Pallas kernels for 0% -> 0%
where the time goes in v1:
time: 366 us; the launch traced here: 360 us
  waiting for transfers between devices  244 us (67%)
  starting transfers between devices  35.3 us (10%)
  matrix products  29.6 us (8%)
  other arithmetic  26.8 us (7%)
  local copies, waits for them, and re-layouts  22.9 us (6%)
    ppermute x10, waiting for transfers between devices, passed_along(): lax.ppermute(x, axis, [(i, (i + by) % devices) for i in range(devices)])  187 us
    all_to_all x2, waiting for transfers between devices, body(): whole = lax.all_to_all(flat, 'lon', split_axis=0, concat_axis=1, tiled=True)  31.9 us
    ppermute x14, waiting for transfers between devices, body(): lax.ppermute(sent, 'lon', [(d, (d + far) % ways) for d in range(ways)])  21.6 us
    select_n x22, other arithmetic, roll_digits(): values = jnp.where(taken, moved, values)  11.1 us
    ppermute x14, starting transfers between devices, body(): lax.ppermute(sent, 'lon', [(d, (d + far) % ways) for d in range(ways)])  11 us
    ppermute x10, starting transfers between devices, passed_along(): lax.ppermute(x, axis, [(i, (i + by) % devices) for i in range(devices)])  9.57 us
    all_to_all x2, starting transfers between devices, body(): whole = lax.all_to_all(flat, 'lon', split_axis=0, concat_axis=1, tiled=True)  7.55 us
    all_to_all x8, local copies, waits for them, and re-layouts, body(): whole = lax.all_to_all(flat, 'lon', split_axis=0, concat_axis=1, tiled=True)  7.42 us
  transfers between devices with their start and end apart: 28, of which 23 were waited for; matrix products, arithmetic and copies ran while one was open for 1% of the time, Pallas kernels for 0%

profile of v1, /device:TPU:0, one launch (start us, length us, event | category | flops | bytes accessed | tf_op | source)
XLA Modules:
  0.0 360.0 jit_solution(4594524290744521118)
XLA Ops:
  0.0 3.0 collective-permute-start
  3.0 22.0 %collective-permute-done = f32[5,1,32,1440]{3,2,1,0:T(8,128)S(1)} collective-permute-done((f32[5,1,32,1440]{3,2,1,0:T(8,128)}, f32[5,1,32,1440]{3,2,1,0:T(8,128)S(1)}, u32[]{:S(2)}, u32[]{:S(2)}) %collective-permute-start) | collective-permute-done | bytes 921632 | tf_op jit(solution)/shard_map/ppermute | solution.py:15
  25.7 13.6 %collective-permute-done.1 = f32[5,1,32,1440]{3,2,1,0:T(8,128)S(1)} collective-permute-done((f32[5,1,32,1440]{3,2,1,0:T(8,128)S(1)}, f32[5,1,32,1440]{3,2,1,0:T(8,128)S(1)}, u32[]{:S(2)}, u32[]{:S(2)}) %collective-permute-start.1) | collective-permute-done | bytes 921632 | tf_op jit(solution)/shard_map/ppermute | solution.py:15
  40.4 22.2 %collective-permute-done.2 = f32[5,1,32,1440]{3,2,1,0:T(8,128)S(1)} collective-permute-done((f32[5,1,32,1440]{3,2,1,0:T(8,128)S(1)}, f32[5,1,32,1440]{3,2,1,0:T(8,128)S(1)}, u32[]{:S(2)}, u32[]{:S(2)}) %collective-permute-start.2) | collective-permute-done | bytes 921632 | tf_op jit(solution)/shard_map/ppermute | solution.py:15
  62.8 1.6 collective-permute-start.3
  64.4 19.7 %collective-permute-done.3 = f32[5,1,32,1440]{3,2,1,0:T(8,128)S(1)} collective-permute-done((f32[5,1,32,1440]{3,2,1,0:T(8,128)S(1)}, f32[5,1,32,1440]{3,2,1,0:T(8,128)S(1)}, u32[]{:S(2)}, u32[]{:S(2)}) %collective-permute-start.3) | collective-permute-done | bytes 921632 | tf_op jit(solution)/shard_map/ppermute | solution.py:15
  84.7 14.1 %collective-permute-done.4 = f32[5,1,32,1440]{3,2,1,0:T(8,128)S(1)} collective-permute-done((f32[5,1,32,1440]{3,2,1,0:T(8,128)S(1)}, f32[5,1,32,1440]{3,2,1,0:T(8,128)S(1)}, u32[]{:S(2)}, u32[]{:S(2)}) %collective-permute-start.4) | collective-permute-done | bytes 921632 | tf_op jit(solution)/shard_map/ppermute | solution.py:15
  107.5 3.8 %all-to-all-start = ((f32[8,20,1440]{2,1,0:T(8,128)}), f32[8,20,1440]{2,1,0:T(8,128)S(1)}, u32[]{:S(2)}, u32[]{:S(2)}) async-start(f32[8,20,1440]{2,1,0:T(8,128)} %all_to_all.32), calls=%async_computation | async-start | bytes 2359296 | tf_op jit(solution)/shard_map/all_to_all | solution.py:152
  112.3 15.6 %all-to-all-done = f32[8,20,1440]{2,1,0:T(8,128)S(1)} async-done(((f32[8,20,1440]{2,1,0:T(8,128)}), f32[8,20,1440]{2,1,0:T(8,128)S(1)}, u32[]{:S(2)}, u32[]{:S(2)}) %all-to-all-start) | async-done | bytes 921632 | tf_op jit(solution)/shard_map/all_to_all | solution.py:152
  129.0 1.4 all_to_all.35
  130.9 1.3 pad_maximum_fusion.5
  132.2 2.4 concatenate.855
  134.7 1.2 concatenate.853
  135.8 2.3 multiply_subtract_fusion.3
  138.1 1.2 convolution_bitcast_fusion.1
  139.3 1.2 fusion.13
  140.5 1.2 fusion.49
  141.7 1.2 fusion.50
  142.9 1.2 fusion.12
  144.1 1.2 fusion.73
  145.2 1.6 fusion.11
  146.9 1.2 fusion.70
  148.1 1.2 convolution_subtract_fusion.4
  149.2 1.2 convolution_add_fusion.2
  150.4 1.3 fusion.37
  151.7 1.3 fusion.10
  155.8 2.6 collective-permute-start.5
  158.4 1.5 collective-permute-start.6
  160.0 3.0 collective-permute-done.10
  163.4 4.8 %collective-permute-done.6 = f32[20,1440]{1,0:T(8,128)S(1)} collective-permute-done((f32[20,1440]{1,0:T(8,128)S(1)}, f32[20,1440]{1,0:T(8,128)S(1)}, u32[]{:S(2)}, u32[]{:S(2)}) %collective-permute-start.6) | collective-permute-done | bytes 115232 | tf_op jit(solution)/shard_map/ppermute | solution.py:161
  168.3 2.8 collective-permute-done.8
  172.2 3.3 collective-permute-start.12
  175.6 1.8 collective-permute-done.12
  178.5 21.8 %collective-permute-done.13 = f32[5,1,32,1440]{3,2,0,1:T(8,128)S(1)} collective-permute-done((f32[5,1,32,1440]{3,2,0,1:T(8,128)S(1)}, f32[5,1,32,1440]{3,2,0,1:T(8,128)S(1)}, u32[]{:S(2)}, u32[]{:S(2)}) %collective-permute-start.13) | collective-permute-done | bytes 921632 | tf_op jit(solution)/shard_map/ppermute | solution.py:15
  200.3 14.4 %collective-permute-done.14 = f32[5,1,32,1440]{3,2,0,1:T(8,128)S(1)} collective-permute-done((f32[5,1,32,1440]{3,2,0,1:T(8,128)S(1)}, f32[5,1,32,1440]{3,2,0,1:T(8,128)S(1)}, u32[]{:S(2)}, u32[]{:S(2)}) %collective-permute-start.14) | collective-permute-done | bytes 921632 | tf_op jit(solution)/shard_map/ppermute | solution.py:15
  214.9 2.8 collective-permute-start.15
  217.7 22.2 %collective-permute-done.15 = f32[5,1,32,1440]{3,2,0,1:T(8,128)S(1)} collective-permute-done((f32[5,1,32,1440]{3,2,0,1:T(8,128)S(1)}, f32[5,1,32,1440]{3,2,0,1:T(8,128)S(1)}, u32[]{:S(2)}, u32[]{:S(2)}) %collective-permute-start.15) | collective-permute-done | bytes 921632 | tf_op jit(solution)/shard_map/ppermute | solution.py:15
  240.6 22.8 %collective-permute-done.16 = f32[5,1,32,1440]{3,2,0,1:T(8,128)S(1)} collective-permute-done((f32[5,1,32,1440]{3,2,0,1:T(8,128)S(1)}, f32[5,1,32,1440]{3,2,0,1:T(8,128)S(1)}, u32[]{:S(2)}, u32[]{:S(2)}) %collective-permute-start.16) | collective-permute-done | bytes 921632 | tf_op jit(solution)/shard_map/ppermute | solution.py:15
  263.9 14.3 %collective-permute-done.17 = f32[5,1,32,1440]{3,2,0,1:T(8,128)S(1)} collective-permute-done((f32[5,1,32,1440]{3,2,0,1:T(8,128)S(1)}, f32[5,1,32,1440]{3,2,0,1:T(8,128)S(1)}, u32[]{:S(2)}, u32[]{:S(2)}) %collective-permute-start.17) | collective-permute-done | bytes 921632 | tf_op jit(solution)/shard_map/ppermute | solution.py:15
  286.9 3.8 %all-to-all-start.1 = ((f32[8,20,1440]{2,1,0:T(8,128)}), f32[8,20,1440]{2,1,0:T(8,128)S(1)}, u32[]{:S(2)}, u32[]{:S(2)}) async-start(f32[8,20,1440]{2,1,0:T(8,128)} %all_to_all.37), calls=%async_computation.1 | async-start | bytes 2359296 | tf_op jit(solution)/shard_map/all_to_all | solution.py:152
  290.9 16.4 %all-to-all-done.1 = f32[8,20,1440]{2,1,0:T(8,128)S(1)} async-done(((f32[8,20,1440]{2,1,0:T(8,128)}), f32[8,20,1440]{2,1,0:T(8,128)S(1)}, u32[]{:S(2)}, u32[]{:S(2)}) %all-to-all-start.1) | async-done | bytes 921632 | tf_op jit(solution)/shard_map/all_to_all | solution.py:152
  308.4 1.4 all_to_all.40
  310.3 1.3 pad_maximum_fusion.7
  311.7 2.4 concatenate.874
  315.2 2.3 multiply_subtract_fusion.1
  317.5 1.2 convolution_bitcast_fusion
  318.7 1.2 fusion.8
  319.9 1.2 fusion.51
  321.1 1.2 fusion.52
  322.3 1.2 fusion.7
  323.5 1.2 fusion.67
  324.6 1.2 fusion.6
  325.9 1.4 fusion.64
  327.3 1.2 convolution_subtract_fusion.1
  328.5 1.2 convolution_add_fusion
  329.6 1.3 fusion.30
  331.0 1.3 fusion.5
  338.7 1.9 collective-permute-start.23
  340.5 1.3 collective-permute-done.19
  342.2 1.4 collective-permute-done.20
  343.6 5.5 %collective-permute-done.21 = f32[20,1440]{1,0:T(8,128)S(1)} collective-permute-done((f32[20,1440]{1,0:T(8,128)S(1)}, f32[20,1440]{1,0:T(8,128)S(1)}, u32[]{:S(2)}, u32[]{:S(2)}) %collective-permute-start.21) | collective-permute-done | bytes 115232 | tf_op jit(solution)/shard_map/ppermute | solution.py:161
  349.1 2.0 collective-permute-done.22
  352.2 4.0 %collective-permute-start.25 = (f32[5,1,2,1440]{3,2,1,0:T(2,128)S(1)}, f32[5,1,2,1440]{3,2,1,0:T(2,128)S(1)}, u32[]{:S(2)}, u32[]{:S(2)}) collective-permute-start(f32[5,1,2,1440]{3,2,1,0:T(2,128)S(1)} %slice.447), channel_id=1, source_target_pairs={{0,1},{1,2},{2,3},{4,5},{5,6},{6,7},{8,9},{9,10},{10,11},{12,13},{... | collective-permute-start | bytes 172808 | tf_op jit(solution)/shard_map/ppermute | solution.py:21
  356.3 1.8 collective-permute-done.25
  (153 shorter events, 41.5 us)
Async XLA Ops:
  0.0 24.9 %collective-permute-start = (f32[5,1,32,1440]{3,2,1,0:T(8,128)}, f32[5,1,32,1440]{3,2,1,0:T(8,128)S(1)}, u32[]{:S(2)}, u32[]{:S(2)}) collective-permute-start(f32[5,1,32,1440]{3,2,1,0:T(8,128)} %param.9), channel_id=1, source_target_pairs={{0,16},{4,20},{8,24},{12,28},{16,0},{20,4},{24,8},{28,12},{1,17},{... | collective-permute-start | bytes 2764808 | tf_op jit(solution)/shard_map/ppermute | solution.py:15
  24.9 14.4 %collective-permute-start.1 = (f32[5,1,32,1440]{3,2,1,0:T(8,128)S(1)}, f32[5,1,32,1440]{3,2,1,0:T(8,128)S(1)}, u32[]{:S(2)}, u32[]{:S(2)}) collective-permute-start(f32[5,1,32,1440]{3,2,1,0:T(8,128)S(1)} %collective-permute-done), channel_id=1, source_target_pairs={{0,4},{4,8},{8,12},{12,16},{16,20},{20,24},{24,28},{28,0},{1,5},{5... | collective-permute-start | bytes 2764808 | tf_op jit(solution)/shard_map/ppermute | solution.py:15
  39.6 23.1 %collective-permute-start.2 = (f32[5,1,32,1440]{3,2,1,0:T(8,128)S(1)}, f32[5,1,32,1440]{3,2,1,0:T(8,128)S(1)}, u32[]{:S(2)}, u32[]{:S(2)}) collective-permute-start(f32[5,1,32,1440]{3,2,1,0:T(8,128)S(1)} %broadcast_select_fusion), channel_id=1, source_target_pairs={{0,8},{4,12},{8,16},{12,20},{16,24},{20,28},{24,0},{28,4},{1,9},{5... | collective-permute-start | bytes 2764808 | tf_op jit(solution)/shard_map/ppermute | solution.py:15
  62.8 21.5 %copy-start.2 = (s32[128]{0:T(128)S(1)}, s32[128]{0:T(128)}, u32[]{:S(2)}) copy-start(s32[128]{0:T(128)} %param.13) | copy-start | bytes 1540
  62.8 21.6 %copy-start = (f32[2,1,128]{2,1,0:T(1,128)S(1)}, f32[2,1,128]{2,1,0:T(1,128)}, u32[]{:S(2)}) copy-start(f32[2,1,128]{2,1,0:T(1,128)} %param.10) | copy-start | bytes 3076
  62.8 21.3 %collective-permute-start.3 = (f32[5,1,32,1440]{3,2,1,0:T(8,128)S(1)}, f32[5,1,32,1440]{3,2,1,0:T(8,128)S(1)}, u32[]{:S(2)}, u32[]{:S(2)}) collective-permute-start(f32[5,1,32,1440]{3,2,1,0:T(8,128)S(1)} %broadcast_select_fusion.1), channel_id=1, source_target_pairs={{0,16},{4,20},{8,24},{12,28},{16,0},{20,4},{24,8},{28,12},{1,17},{... | collective-permute-start | bytes 2764808 | tf_op jit(solution)/shard_map/ppermute | solution.py:15
  84.3 14.5 %collective-permute-start.4 = (f32[5,1,32,1440]{3,2,1,0:T(8,128)S(1)}, f32[5,1,32,1440]{3,2,1,0:T(8,128)S(1)}, u32[]{:S(2)}, u32[]{:S(2)}) collective-permute-start(f32[5,1,32,1440]{3,2,1,0:T(8,128)S(1)} %broadcast_select_fusion.2), channel_id=1, source_target_pairs={{0,4},{4,8},{8,12},{12,16},{16,20},{20,24},{24,28},{28,0},{1,5},{5... | collective-permute-start | bytes 2764808 | tf_op jit(solution)/shard_map/ppermute | solution.py:15
  107.5 20.3 %all-to-all-start = ((f32[8,20,1440]{2,1,0:T(8,128)}), f32[8,20,1440]{2,1,0:T(8,128)S(1)}, u32[]{:S(2)}, u32[]{:S(2)}) async-start(f32[8,20,1440]{2,1,0:T(8,128)} %all_to_all.32), calls=%async_computation | async-start | bytes 2359296 | tf_op jit(solution)/shard_map/all_to_all | solution.py:152
  154.3 9.1 %copy-start.1 = (f32[2,1,128]{2,1,0:T(1,128)S(1)}, f32[2,1,128]{2,1,0:T(1,128)}, u32[]{:S(2)}) copy-start(f32[2,1,128]{2,1,0:T(1,128)} %param.11) | copy-start | bytes 3076
  155.2 7.7 %collective-permute-start.10 = (f32[20,1440]{1,0:T(8,128)S(1)}, f32[20,1440]{1,0:T(8,128)S(1)}, u32[]{:S(2)}, u32[]{:S(2)}) collective-permute-start(f32[20,1440]{1,0:T(8,128)S(1)} %get-tuple-element.35), channel_id=1, source_target_pairs={{0,8},{4,12},{8,16},{12,20},{16,24},{20,28},{24,0},{28,4},{1,9},{5... | collective-permute-start | bytes 345608 | tf_op jit(solution)/shard_map/ppermute | solution.py:161
  155.8 7.6 %collective-permute-start.11 = (f32[20,1440]{1,0:T(8,128)S(1)}, f32[20,1440]{1,0:T(8,128)S(1)}, u32[]{:S(2)}, u32[]{:S(2)}) collective-permute-start(f32[20,1440]{1,0:T(8,128)S(1)} %get-tuple-element.34), channel_id=1, source_target_pairs={{0,4},{4,8},{8,12},{12,16},{16,20},{20,24},{24,28},{28,0},{1,5},{5... | collective-permute-start | bytes 345608 | tf_op jit(solution)/shard_map/ppermute | solution.py:161
  155.8 7.6 %collective-permute-start.5 = (f32[20,1440]{1,0:T(8,128)S(1)}, f32[20,1440]{1,0:T(8,128)S(1)}, u32[]{:S(2)}, u32[]{:S(2)}) collective-permute-start(f32[20,1440]{1,0:T(8,128)S(1)} %get-tuple-element.40), channel_id=1, source_target_pairs={{0,28},{4,0},{8,4},{12,8},{16,12},{20,16},{24,20},{28,24},{1,29},{... | collective-permute-start | bytes 345608 | tf_op jit(solution)/shard_map/ppermute | solution.py:161
  158.4 9.8 %collective-permute-start.6 = (f32[20,1440]{1,0:T(8,128)S(1)}, f32[20,1440]{1,0:T(8,128)S(1)}, u32[]{:S(2)}, u32[]{:S(2)}) collective-permute-start(f32[20,1440]{1,0:T(8,128)S(1)} %get-tuple-element.39), channel_id=1, source_target_pairs={{0,24},{4,28},{8,0},{12,4},{16,8},{20,12},{24,16},{28,20},{1,25},{... | collective-permute-start | bytes 345608 | tf_op jit(solution)/shard_map/ppermute | solution.py:161
  160.0 8.4 %collective-permute-start.7 = (f32[20,1440]{1,0:T(8,128)S(1)}, f32[20,1440]{1,0:T(8,128)S(1)}, u32[]{:S(2)}, u32[]{:S(2)}) collective-permute-start(f32[20,1440]{1,0:T(8,128)S(1)} %get-tuple-element.38), channel_id=1, source_target_pairs={{0,20},{4,24},{8,28},{12,0},{16,4},{20,8},{24,12},{28,16},{1,21},{... | collective-permute-start | bytes 345608 | tf_op jit(solution)/shard_map/ppermute | solution.py:161
  162.9 8.2 %collective-permute-start.8 = (f32[20,1440]{1,0:T(8,128)S(1)}, f32[20,1440]{1,0:T(8,128)S(1)}, u32[]{:S(2)}, u32[]{:S(2)}) collective-permute-start(f32[20,1440]{1,0:T(8,128)S(1)} %get-tuple-element.37), channel_id=1, source_target_pairs={{0,16},{4,20},{8,24},{12,28},{16,0},{20,4},{24,8},{28,12},{1,17},{... | collective-permute-start | bytes 345608 | tf_op jit(solution)/shard_map/ppermute | solution.py:161
  163.4 7.7 %collective-permute-start.9 = (f32[20,1440]{1,0:T(8,128)S(1)}, f32[20,1440]{1,0:T(8,128)S(1)}, u32[]{:S(2)}, u32[]{:S(2)}) collective-permute-start(f32[20,1440]{1,0:T(8,128)S(1)} %get-tuple-element.36), channel_id=1, source_target_pairs={{0,12},{4,16},{8,20},{12,24},{16,28},{20,0},{24,4},{28,8},{1,13},{... | collective-permute-start | bytes 345608 | tf_op jit(solution)/shard_map/ppermute | solution.py:161
  172.2 5.1 %collective-permute-start.12 = (f32[5,1,2,1440]{3,2,0,1:T(2,128)S(1)}, f32[5,1,2,1440]{3,2,0,1:T(2,128)S(1)}, u32[]{:S(2)}, u32[]{:S(2)}) collective-permute-start(f32[5,1,2,1440]{3,2,0,1:T(2,128)S(1)} %slice.406), channel_id=1, source_target_pairs={{0,1},{1,2},{2,3},{4,5},{5,6},{6,7},{8,9},{9,10},{10,11},{12,13},{... | collective-permute-start | bytes 172808 | tf_op jit(solution)/shard_map/ppermute | solution.py:21
  177.9 22.4 %collective-permute-start.13 = (f32[5,1,32,1440]{3,2,0,1:T(8,128)S(1)}, f32[5,1,32,1440]{3,2,0,1:T(8,128)S(1)}, u32[]{:S(2)}, u32[]{:S(2)}) collective-permute-start(f32[5,1,32,1440]{3,2,0,1:T(8,128)S(1)} %slice_subtract_fusion.1), channel_id=1, source_target_pairs={{0,16},{4,20},{8,24},{12,28},{16,0},{20,4},{24,8},{28,12},{1,17},{... | collective-permute-start | bytes 2764808 | tf_op jit(solution)/shard_map/ppermute | solution.py:15
  200.3 14.4 %collective-permute-start.14 = (f32[5,1,32,1440]{3,2,0,1:T(8,128)S(1)}, f32[5,1,32,1440]{3,2,0,1:T(8,128)S(1)}, u32[]{:S(2)}, u32[]{:S(2)}) collective-permute-start(f32[5,1,32,1440]{3,2,0,1:T(8,128)S(1)} %collective-permute-done.13), channel_id=1, source_target_pairs={{0,4},{4,8},{8,12},{12,16},{16,20},{20,24},{24,28},{28,0},{1,5},{5... | collective-permute-start | bytes 2764808 | tf_op jit(solution)/shard_map/ppermute | solution.py:15
  214.9 25.0 %collective-permute-start.15 = (f32[5,1,32,1440]{3,2,0,1:T(8,128)S(1)}, f32[5,1,32,1440]{3,2,0,1:T(8,128)S(1)}, u32[]{:S(2)}, u32[]{:S(2)}) collective-permute-start(f32[5,1,32,1440]{3,2,0,1:T(8,128)S(1)} %broadcast_select_fusion.3), channel_id=1, source_target_pairs={{0,8},{4,12},{8,16},{12,20},{16,24},{20,28},{24,0},{28,4},{1,9},{5... | collective-permute-start | bytes 2764808 | tf_op jit(solution)/shard_map/ppermute | solution.py:15
  240.1 23.3 %collective-permute-start.16 = (f32[5,1,32,1440]{3,2,0,1:T(8,128)S(1)}, f32[5,1,32,1440]{3,2,0,1:T(8,128)S(1)}, u32[]{:S(2)}, u32[]{:S(2)}) collective-permute-start(f32[5,1,32,1440]{3,2,0,1:T(8,128)S(1)} %broadcast_select_fusion.4), channel_id=1, source_target_pairs={{0,16},{4,20},{8,24},{12,28},{16,0},{20,4},{24,8},{28,12},{1,17},{... | collective-permute-start | bytes 2764808 | tf_op jit(solution)/shard_map/ppermute | solution.py:15
  263.6 14.6 %collective-permute-start.17 = (f32[5,1,32,1440]{3,2,0,1:T(8,128)S(1)}, f32[5,1,32,1440]{3,2,0,1:T(8,128)S(1)}, u32[]{:S(2)}, u32[]{:S(2)}) collective-permute-start(f32[5,1,32,1440]{3,2,0,1:T(8,128)S(1)} %broadcast_select_fusion.5), channel_id=1, source_target_pairs={{0,4},{4,8},{8,12},{12,16},{16,20},{20,24},{24,28},{28,0},{1,5},{5... | collective-permute-start | bytes 2764808 | tf_op jit(solution)/shard_map/ppermute | solution.py:15
  286.9 20.3 %all-to-all-start.1 = ((f32[8,20,1440]{2,1,0:T(8,128)}), f32[8,20,1440]{2,1,0:T(8,128)S(1)}, u32[]{:S(2)}, u32[]{:S(2)}) async-start(f32[8,20,1440]{2,1,0:T(8,128)} %all_to_all.37), calls=%async_computation.1 | async-start | bytes 2359296 | tf_op jit(solution)/shard_map/all_to_all | solution.py:152
  334.4 4.2 %collective-permute-start.18 = (f32[20,1440]{1,0:T(8,128)S(1)}, f32[20,1440]{1,0:T(8,128)S(1)}, u32[]{:S(2)}, u32[]{:S(2)}) collective-permute-start(f32[20,1440]{1,0:T(8,128)S(1)} %get-tuple-element.32), channel_id=1, source_target_pairs={{0,28},{4,0},{8,4},{12,8},{16,12},{20,16},{24,20},{28,24},{1,29},{... | collective-permute-start | bytes 345608 | tf_op jit(solution)/shard_map/ppermute | solution.py:161
  334.5 7.3 %collective-permute-start.19 = (f32[20,1440]{1,0:T(8,128)S(1)}, f32[20,1440]{1,0:T(8,128)S(1)}, u32[]{:S(2)}, u32[]{:S(2)}) collective-permute-start(f32[20,1440]{1,0:T(8,128)S(1)} %get-tuple-element.31), channel_id=1, source_target_pairs={{0,24},{4,28},{8,0},{12,4},{16,8},{20,12},{24,16},{28,20},{1,25},{... | collective-permute-start | bytes 345608 | tf_op jit(solution)/shard_map/ppermute | solution.py:161
  335.2 8.4 %collective-permute-start.20 = (f32[20,1440]{1,0:T(8,128)S(1)}, f32[20,1440]{1,0:T(8,128)S(1)}, u32[]{:S(2)}, u32[]{:S(2)}) collective-permute-start(f32[20,1440]{1,0:T(8,128)S(1)} %get-tuple-element.30), channel_id=1, source_target_pairs={{0,20},{4,24},{8,28},{12,0},{16,4},{20,8},{24,12},{28,16},{1,21},{... | collective-permute-start | bytes 345608 | tf_op jit(solution)/shard_map/ppermute | solution.py:161
  336.3 12.8 %collective-permute-start.21 = (f32[20,1440]{1,0:T(8,128)S(1)}, f32[20,1440]{1,0:T(8,128)S(1)}, u32[]{:S(2)}, u32[]{:S(2)}) collective-permute-start(f32[20,1440]{1,0:T(8,128)S(1)} %get-tuple-element.29), channel_id=1, source_target_pairs={{0,16},{4,20},{8,24},{12,28},{16,0},{20,4},{24,8},{28,12},{1,17},{... | collective-permute-start | bytes 345608 | tf_op jit(solution)/shard_map/ppermute | solution.py:161
  337.0 14.2 %collective-permute-start.22 = (f32[20,1440]{1,0:T(8,128)S(1)}, f32[20,1440]{1,0:T(8,128)S(1)}, u32[]{:S(2)}, u32[]{:S(2)}) collective-permute-start(f32[20,1440]{1,0:T(8,128)S(1)} %get-tuple-element.28), channel_id=1, source_target_pairs={{0,12},{4,16},{8,20},{12,24},{16,28},{20,0},{24,4},{28,8},{1,13},{... | collective-permute-start | bytes 345608 | tf_op jit(solution)/shard_map/ppermute | solution.py:161
  338.7 12.5 %collective-permute-start.23 = (f32[20,1440]{1,0:T(8,128)S(1)}, f32[20,1440]{1,0:T(8,128)S(1)}, u32[]{:S(2)}, u32[]{:S(2)}) collective-permute-start(f32[20,1440]{1,0:T(8,128)S(1)} %get-tuple-element.27), channel_id=1, source_target_pairs={{0,8},{4,12},{8,16},{12,20},{16,24},{20,28},{24,0},{28,4},{1,9},{5... | collective-permute-start | bytes 345608 | tf_op jit(solution)/shard_map/ppermute | solution.py:161
  341.8 9.3 %collective-permute-start.24 = (f32[20,1440]{1,0:T(8,128)S(1)}, f32[20,1440]{1,0:T(8,128)S(1)}, u32[]{:S(2)}, u32[]{:S(2)}) collective-permute-start(f32[20,1440]{1,0:T(8,128)S(1)} %get-tuple-element.26), channel_id=1, source_target_pairs={{0,4},{4,8},{8,12},{12,16},{16,20},{20,24},{24,28},{28,0},{1,5},{5... | collective-permute-start | bytes 345608 | tf_op jit(solution)/shard_map/ppermute | solution.py:161
  352.2 5.8 %collective-permute-start.25 = (f32[5,1,2,1440]{3,2,1,0:T(2,128)S(1)}, f32[5,1,2,1440]{3,2,1,0:T(2,128)S(1)}, u32[]{:S(2)}, u32[]{:S(2)}) collective-permute-start(f32[5,1,2,1440]{3,2,1,0:T(2,128)S(1)} %slice.447), channel_id=1, source_target_pairs={{0,1},{1,2},{2,3},{4,5},{5,6},{6,7},{8,9},{9,10},{10,11},{12,13},{... | collective-permute-start | bytes 172808 | tf_op jit(solution)/shard_map/ppermute | solution.py:21
